TPU v7x, 256 devices: a whole 4x4x8 slice. The times are simulated.
256 devices in a mesh: dom: 8 (over x, core), st: 32 (over y, z).
Axes of the slice: x: 4, y: 4, z: 8, core: 2. Of those that a mesh axis runs over, the one named last changes fastest.
Arguments:
- orbitals: bfloat16 [512, 512, 1024], P('st', 'dom'), may hold values from -6 to 6
- potential: bfloat16 [512, 1024], P('dom'), may hold values from -0.5 to 0.5
- rotation: bfloat16 [512, 512], P('st'), may hold values from -0.25 to 0.25
Outputs:
- rotated: bfloat16 [512, 524288], P(None, ('dom', 'st'))
All inputs are finite; a program needn't handle non-finite values.
Results may differ from a plain program's by a relative error of at most 0.0049.
Values may be sent and summed in bfloat16 or wider, within the bound.
No kernel may reach another device: no remote copies, remote signals or barrier semaphores. Data moves between devices by JAX's collectives and lax.ppermute only.
A program may use at most 64 MiB of HBM per device.

v0:
```python
import jax
import jax.numpy as jnp
from jax import lax
from jax.sharding import PartitionSpec as P

DEGREE = 4
NZ = 32
cheb_shift = 3.75
cheb_scale = 3.25


def extended(block, sides, width):
    for axis, dim in sides:
        count = lax.axis_size(axis)
        forward = [(i, i + 1) for i in range(count - 1)]
        backward = [(target, source) for source, target in forward]
        low = lax.ppermute(
            lax.slice_in_dim(block, block.shape[dim] - width, None, axis=dim), axis, forward
        )
        high = lax.ppermute(lax.slice_in_dim(block, 0, width, axis=dim), axis, backward)
        block = jnp.concatenate([low, block, high], axis=dim)
    return block


def neighbour_sum(center, nz_count):
    row_width = center.shape[2]
    z_position = lax.broadcasted_iota(jnp.int32, (1, 1, row_width), 2) % nz_count
    padded = jnp.pad(center, ((0, 0), (0, 0), (nz_count, nz_count)))
    along_y = padded[:, :, 2 * nz_count :] + padded[:, :, :row_width]
    upper_z = jnp.where(
        z_position < nz_count - 1, padded[:, :, nz_count + 1 : nz_count + 1 + row_width], 0.0
    )
    lower_z = jnp.where(z_position > 0, padded[:, :, nz_count - 1 : nz_count - 1 + row_width], 0.0)
    return along_y + upper_z + lower_z


def hamiltonian(padded_x, local_pot, nz_count):
    center = padded_x[:, 1:-1]
    beside = padded_x[:, 2:] + padded_x[:, :-2] + neighbour_sum(center, nz_count)
    return (3.0 + local_pot) * center - 0.5 * beside


def chebyshev(start, apply_fn, degree):
    previous = start
    current = (apply_fn(start) - cheb_shift * start) / cheb_scale
    for filter_order in range(1, degree):
        following = 2.0 * (apply_fn(current) - cheb_shift * current) / cheb_scale - previous
        previous = current
        current = following
    return current


def local(orbitals, potential, rotation):
    start = orbitals.astype(jnp.float32)
    local_pot = potential.astype(jnp.float32)
    states_dev, planes, row_width = start.shape

    def apply_step(state_field):
        padded = extended(state_field, (("dom", 1),), 1)
        return hamiltonian(padded, local_pot, NZ)

    result = chebyshev(start, apply_step, DEGREE)
    filtered = result.astype(jnp.bfloat16).reshape(states_dev, planes * row_width)
    regrouped = lax.all_to_all(filtered, "st", split_axis=1, concat_axis=0, tiled=True)
    product = jnp.dot(
        lax.all_gather(rotation, "st", axis=0, tiled=True),
        regrouped,
        preferred_element_type=jnp.float32,
    )
    return product.astype(jnp.bfloat16)


def solution(mesh):
    return jax.shard_map(
        local,
        mesh=mesh,
        in_specs=(P("st", "dom", None), P("dom", None), P("st", None)),
        out_specs=P(None, ("dom", "st")),
        check_vma=False,
    )
```

profile of v0, /device:TPU:2, one launch (start us, length us, event | category | flops | bytes accessed | tf_op | source)
XLA Modules:
  0.0 166.8 jit_solution(14921552852424381821)
XLA Ops:
  0.0 1.1 fusion.57
  1.2 1.9 %collective-permute-start = (f32[16,1,1024]{2,1,0:T(1,128)S(1)}, f32[16,1,1024]{2,1,0:T(1,128)S(1)}, u32[]{:S(2)}, u32[]{:S(2)}) collective-permute-start(f32[16,1,1024]{2,1,0:T(1,128)S(1)} %get-tuple-element.13), channel_id=1, source_target_pairs={{32,0},{64,32},{96,64},{128,96},{160,128},{192,160},{224,192},{33,... | collective-permute-start | bytes 196616 | tf_op jit(solution)/shard_map/ppermute | solution.py:20
  3.1 2.4 %collective-permute-start.1 = (f32[16,1,1024]{2,1,0:T(1,128)S(1)}, f32[16,1,1024]{2,1,0:T(1,128)S(1)}, u32[]{:S(2)}, u32[]{:S(2)}) collective-permute-start(f32[16,1,1024]{2,1,0:T(1,128)S(1)} %get-tuple-element.14), channel_id=1, source_target_pairs={{0,32},{32,64},{64,96},{96,128},{128,160},{160,192},{192,224},{1,3... | collective-permute-start | bytes 196616 | tf_op jit(solution)/shard_map/ppermute | solution.py:17
  5.5 2.0 %convert_element_type.21 = f32[16,64,1024]{2,1,0:T(8,128)S(1)} convert(bf16[16,64,1024]{2,1,0:T(8,128)(2,1)} %param.3) | non-fusion elementwise | flops 1048576 | bytes 6291456 | tf_op jit(solution)/shard_map/convert_element_type | solution.py:54
  7.6 1.6 collective-permute-done.1
  9.3 4.7 %broadcast_multiply_fusion = (f32[16,64,1024]{2,1,0:T(8,128)S(1)}, f32[16,64,1024]{2,1,0:T(8,128)S(1)}) fusion(f32[16,64,1024]{2,1,0:T(8,128)S(1)} %convert_element_type.21, pred[1024]{0:T(1024)(128)(4,1)S(1)} %get-tuple-element.17, pred[1024]{0:T(1024)(128)(4,1)S(1)} %get-tuple-element.18, f32[16,1,1024]{2,1,0:T(1,128)S(1)} %collective-permute-done.1, ...), kind=kLoop, calls=%fused_computation.73 | loop fusion | flops 15728640 | bytes 12978176 | tf_op jit(solution)/shard_map/div | solution.py:45
  14.0 2.2 %collective-permute-start.2 = (f32[16,1,1024]{2,1,0:T(1,128)S(1)}, f32[16,1,1024]{2,1,0:T(1,128)S(1)}, u32[]{:S(2)}, u32[]{:S(2)}) collective-permute-start(f32[16,1,1024]{2,1,0:T(1,128)S(1)} %get-tuple-element.11), channel_id=1, source_target_pairs={{32,0},{64,32},{96,64},{128,96},{160,128},{192,160},{224,192},{33,... | collective-permute-start | bytes 196616 | tf_op jit(solution)/shard_map/ppermute | solution.py:20
  16.2 2.2 %collective-permute-start.3 = (f32[16,1,1024]{2,1,0:T(1,128)S(1)}, f32[16,1,1024]{2,1,0:T(1,128)S(1)}, u32[]{:S(2)}, u32[]{:S(2)}) collective-permute-start(f32[16,1,1024]{2,1,0:T(1,128)S(1)} %get-tuple-element.12), channel_id=1, source_target_pairs={{0,32},{32,64},{64,96},{96,128},{128,160},{160,192},{192,224},{1,3... | collective-permute-start | bytes 196616 | tf_op jit(solution)/shard_map/ppermute | solution.py:17
  18.4 3.4 %collective-permute-done.3 = f32[16,1,1024]{2,1,0:T(1,128)S(1)} collective-permute-done((f32[16,1,1024]{2,1,0:T(1,128)S(1)}, f32[16,1,1024]{2,1,0:T(1,128)S(1)}, u32[]{:S(2)}, u32[]{:S(2)}) %collective-permute-start.3) | collective-permute-done | bytes 65568 | tf_op jit(solution)/shard_map/ppermute | solution.py:17
  21.8 6.1 %fusion.17 = f32[16,64,1024]{2,1,0:T(8,128)S(1)} fusion(f32[16,64,1024]{2,1,0:T(8,128)S(1)} %get-tuple-element.5, f32[16,1,1024]{2,1,0:T(1,128)S(1)} %collective-permute-done.3, f32[16,1,1024]{2,1,0:T(1,128)S(1)} %collective-permute-done.2, f32[16,64,1024]{2,1,0:T(8,128)S(1)} %get-tuple-element.6, f32[64,1024]{1,0:T(8,128)S(1)} %get-tuple-element.15, ...), kind=kLoop, calls=%fused_computation.33 | loop fusion | flops 17825792 | bytes 15075328 | tf_op jit(solution)/shard_map/sub | solution.py:47
  28.0 1.9 %collective-permute-start.4 = (f32[16,1,1024]{2,1,0:T(1,128)S(1)}, f32[16,1,1024]{2,1,0:T(1,128)S(1)}, u32[]{:S(2)}, u32[]{:S(2)}) collective-permute-start(f32[16,1,1024]{2,1,0:T(1,128)S(1)} %get-tuple-element.9), channel_id=1, source_target_pairs={{32,0},{64,32},{96,64},{128,96},{160,128},{192,160},{224,192},{33,... | collective-permute-start | bytes 196616 | tf_op jit(solution)/shard_map/ppermute | solution.py:20
  30.0 2.4 %collective-permute-start.5 = (f32[16,1,1024]{2,1,0:T(1,128)S(1)}, f32[16,1,1024]{2,1,0:T(1,128)S(1)}, u32[]{:S(2)}, u32[]{:S(2)}) collective-permute-start(f32[16,1,1024]{2,1,0:T(1,128)S(1)} %get-tuple-element.10), channel_id=1, source_target_pairs={{0,32},{32,64},{64,96},{96,128},{128,160},{160,192},{192,224},{1,3... | collective-permute-start | bytes 196616 | tf_op jit(solution)/shard_map/ppermute | solution.py:17
  32.4 3.2 %collective-permute-done.5 = f32[16,1,1024]{2,1,0:T(1,128)S(1)} collective-permute-done((f32[16,1,1024]{2,1,0:T(1,128)S(1)}, f32[16,1,1024]{2,1,0:T(1,128)S(1)}, u32[]{:S(2)}, u32[]{:S(2)}) %collective-permute-start.5) | collective-permute-done | bytes 65568 | tf_op jit(solution)/shard_map/ppermute | solution.py:17
  35.6 4.7 %fusion.28 = f32[16,64,1024]{2,1,0:T(8,128)S(1)} fusion(f32[16,64,1024]{2,1,0:T(8,128)S(1)} %fusion.17, f32[16,1,1024]{2,1,0:T(1,128)S(1)} %collective-permute-done.5, f32[16,1,1024]{2,1,0:T(1,128)S(1)} %collective-permute-done.4, f32[16,64,1024]{2,1,0:T(8,128)S(1)} %get-tuple-element.6, f32[64,1024]{1,0:T(8,128)S(1)} %get-tuple-element.16, ...), kind=kLoop, calls=%fused_computation.44 | loop fusion | flops 17825792 | bytes 12978176 | tf_op jit(solution)/shard_map/sub | solution.py:47
  40.4 1.9 %collective-permute-start.6 = (f32[16,1,1024]{2,1,0:T(1,128)S(1)}, f32[16,1,1024]{2,1,0:T(1,128)S(1)}, u32[]{:S(2)}, u32[]{:S(2)}) collective-permute-start(f32[16,1,1024]{2,1,0:T(1,128)S(1)} %get-tuple-element.7), channel_id=1, source_target_pairs={{32,0},{64,32},{96,64},{128,96},{160,128},{192,160},{224,192},{33,... | collective-permute-start | bytes 196616 | tf_op jit(solution)/shard_map/ppermute | solution.py:20
  42.3 2.6 %collective-permute-start.7 = (f32[16,1,1024]{2,1,0:T(1,128)S(1)}, f32[16,1,1024]{2,1,0:T(1,128)S(1)}, u32[]{:S(2)}, u32[]{:S(2)}) collective-permute-start(f32[16,1,1024]{2,1,0:T(1,128)S(1)} %get-tuple-element.8), channel_id=1, source_target_pairs={{0,32},{32,64},{64,96},{96,128},{128,160},{160,192},{192,224},{1,3... | collective-permute-start | bytes 196616 | tf_op jit(solution)/shard_map/ppermute | solution.py:17
  44.9 3.0 %collective-permute-done.7 = f32[16,1,1024]{2,1,0:T(1,128)S(1)} collective-permute-done((f32[16,1,1024]{2,1,0:T(1,128)S(1)}, f32[16,1,1024]{2,1,0:T(1,128)S(1)}, u32[]{:S(2)}, u32[]{:S(2)}) %collective-permute-start.7) | collective-permute-done | bytes 65568 | tf_op jit(solution)/shard_map/ppermute | solution.py:17
  47.9 5.8 %fusion.40 = bf16[16,64,1024]{2,1,0:T(8,128)(2,1)} fusion(f32[16,64,1024]{2,1,0:T(8,128)S(1)} %fusion.17, f32[16,64,1024]{2,1,0:T(8,128)S(1)} %fusion.28, f32[16,1,1024]{2,1,0:T(1,128)S(1)} %collective-permute-done.7, f32[16,1,1024]{2,1,0:T(1,128)S(1)} %collective-permute-done.6, f32[64,1024]{1,0:T(8,128)S(1)} %get-tuple-element.16, ...), kind=kLoop, calls=%fused_computation.56 | loop fusion | flops 17825792 | bytes 10881024 | tf_op jit(solution)/shard_map/convert_element_type | solution.py:63
  53.7 2.7 %all_to_all.14 = bf16[16,32,2048]{2,1,0:T(8,128)(2,1)S(1)} reshape(bf16[16,64,1024]{2,1,0:T(8,128)(2,1)} %fusion.40) | data formatting | bytes 4194304 | tf_op jit(solution)/shard_map/all_to_all | solution.py:64
  56.4 2.5 %copy.8 = bf16[16,32,2048]{2,0,1:T(8,128)(2,1)} copy(bf16[16,32,2048]{2,1,0:T(8,128)(2,1)S(1)} %all_to_all.14) | data formatting | bytes 4194304 | tf_op jit(solution)/shard_map/all_to_all | solution.py:64
  58.8 10.9 %all-to-all-start = ((bf16[16,32,2048]{2,0,1:T(8,128)(2,1)}), bf16[16,32,2048]{2,0,1:T(8,128)(2,1)S(1)}, u32[]{:S(2)}, u32[]{:S(2)}) async-start(bf16[16,32,2048]{2,0,1:T(8,128)(2,1)} %copy.8), calls=%async_computation | async-start | bytes 4194304 | tf_op jit(solution)/shard_map/all_to_all | solution.py:64
  69.7 90.6 %all_gather.3 = bf16[512,512]{1,0:T(8,128)(2,1)S(1)} all-gather(bf16[16,512]{1,0:T(8,128)(2,1)S(1)} %copy-done.1), channel_id=1, replica_groups=mesh['dom'=8,'st'=32] {'st'}, dimensions={0}, use_global_device_ids=true | all-gather | bytes 540672 | tf_op jit(solution)/shard_map/all_gather | solution.py:66
  160.3 2.7 %fusion.47 = bf16[512,2048]{0,1:T(8,128)(2,1)} fusion(bf16[512,2048]{1,0:T(8,128)(2,1)S(1)} %bitcast.7, bf16[512,512]{1,0:T(8,128)(2,1)S(1)} %all_gather.3), kind=kOutput, calls=%fused_computation.72 | convolution fusion | flops 1074790400 | bytes 4718592 | tf_op jit(solution)/shard_map/dot_general | solution.py:65
  162.9 3.9 %copy.9 = bf16[512,2048]{1,0:T(8,128)(2,1)} copy(bf16[512,2048]{0,1:T(8,128)(2,1)} %fusion.47) | data formatting | bytes 4194304 | tf_op jit(solution)/shard_map/convert_element_type | solution.py:70
  (14 shorter events, 0.4 us)
Async XLA Ops:
  0.0 7.6 %copy-start = (bf16[64,1024]{1,0:T(8,128)(2,1)S(1)}, bf16[64,1024]{1,0:T(8,128)(2,1)}, u32[]{:S(2)}) copy-start(bf16[64,1024]{1,0:T(8,128)(2,1)} %param.4) | copy-start | bytes 393220
  1.2 6.5 %collective-permute-start = (f32[16,1,1024]{2,1,0:T(1,128)S(1)}, f32[16,1,1024]{2,1,0:T(1,128)S(1)}, u32[]{:S(2)}, u32[]{:S(2)}) collective-permute-start(f32[16,1,1024]{2,1,0:T(1,128)S(1)} %get-tuple-element.13), channel_id=1, source_target_pairs={{32,0},{64,32},{96,64},{128,96},{160,128},{192,160},{224,192},{33,... | collective-permute-start | bytes 196616 | tf_op jit(solution)/shard_map/ppermute | solution.py:20
  3.1 6.2 %collective-permute-start.1 = (f32[16,1,1024]{2,1,0:T(1,128)S(1)}, f32[16,1,1024]{2,1,0:T(1,128)S(1)}, u32[]{:S(2)}, u32[]{:S(2)}) collective-permute-start(f32[16,1,1024]{2,1,0:T(1,128)S(1)} %get-tuple-element.14), channel_id=1, source_target_pairs={{0,32},{32,64},{64,96},{96,128},{128,160},{160,192},{192,224},{1,3... | collective-permute-start | bytes 196616 | tf_op jit(solution)/shard_map/ppermute | solution.py:17
  14.0 4.3 %collective-permute-start.2 = (f32[16,1,1024]{2,1,0:T(1,128)S(1)}, f32[16,1,1024]{2,1,0:T(1,128)S(1)}, u32[]{:S(2)}, u32[]{:S(2)}) collective-permute-start(f32[16,1,1024]{2,1,0:T(1,128)S(1)} %get-tuple-element.11), channel_id=1, source_target_pairs={{32,0},{64,32},{96,64},{128,96},{160,128},{192,160},{224,192},{33,... | collective-permute-start | bytes 196616 | tf_op jit(solution)/shard_map/ppermute | solution.py:20
  16.2 5.6 %collective-permute-start.3 = (f32[16,1,1024]{2,1,0:T(1,128)S(1)}, f32[16,1,1024]{2,1,0:T(1,128)S(1)}, u32[]{:S(2)}, u32[]{:S(2)}) collective-permute-start(f32[16,1,1024]{2,1,0:T(1,128)S(1)} %get-tuple-element.12), channel_id=1, source_target_pairs={{0,32},{32,64},{64,96},{96,128},{128,160},{160,192},{192,224},{1,3... | collective-permute-start | bytes 196616 | tf_op jit(solution)/shard_map/ppermute | solution.py:17
  28.0 4.3 %collective-permute-start.4 = (f32[16,1,1024]{2,1,0:T(1,128)S(1)}, f32[16,1,1024]{2,1,0:T(1,128)S(1)}, u32[]{:S(2)}, u32[]{:S(2)}) collective-permute-start(f32[16,1,1024]{2,1,0:T(1,128)S(1)} %get-tuple-element.9), channel_id=1, source_target_pairs={{32,0},{64,32},{96,64},{128,96},{160,128},{192,160},{224,192},{33,... | collective-permute-start | bytes 196616 | tf_op jit(solution)/shard_map/ppermute | solution.py:20
  30.0 5.6 %collective-permute-start.5 = (f32[16,1,1024]{2,1,0:T(1,128)S(1)}, f32[16,1,1024]{2,1,0:T(1,128)S(1)}, u32[]{:S(2)}, u32[]{:S(2)}) collective-permute-start(f32[16,1,1024]{2,1,0:T(1,128)S(1)} %get-tuple-element.10), channel_id=1, source_target_pairs={{0,32},{32,64},{64,96},{96,128},{128,160},{160,192},{192,224},{1,3... | collective-permute-start | bytes 196616 | tf_op jit(solution)/shard_map/ppermute | solution.py:17
  40.4 4.5 %collective-permute-start.6 = (f32[16,1,1024]{2,1,0:T(1,128)S(1)}, f32[16,1,1024]{2,1,0:T(1,128)S(1)}, u32[]{:S(2)}, u32[]{:S(2)}) collective-permute-start(f32[16,1,1024]{2,1,0:T(1,128)S(1)} %get-tuple-element.7), channel_id=1, source_target_pairs={{32,0},{64,32},{96,64},{128,96},{160,128},{192,160},{224,192},{33,... | collective-permute-start | bytes 196616 | tf_op jit(solution)/shard_map/ppermute | solution.py:20
  42.3 5.6 %collective-permute-start.7 = (f32[16,1,1024]{2,1,0:T(1,128)S(1)}, f32[16,1,1024]{2,1,0:T(1,128)S(1)}, u32[]{:S(2)}, u32[]{:S(2)}) collective-permute-start(f32[16,1,1024]{2,1,0:T(1,128)S(1)} %get-tuple-element.8), channel_id=1, source_target_pairs={{0,32},{32,64},{64,96},{96,128},{128,160},{160,192},{192,224},{1,3... | collective-permute-start | bytes 196616 | tf_op jit(solution)/shard_map/ppermute | solution.py:17
  56.3 13.4 %copy-start.1 = (bf16[16,512]{1,0:T(8,128)(2,1)S(1)}, bf16[16,512]{1,0:T(8,128)(2,1)}, u32[]{:S(2)}) copy-start(bf16[16,512]{1,0:T(8,128)(2,1)} %param.5) | copy-start | bytes 49156
  58.8 101.5 %all-to-all-start = ((bf16[16,32,2048]{2,0,1:T(8,128)(2,1)}), bf16[16,32,2048]{2,0,1:T(8,128)(2,1)S(1)}, u32[]{:S(2)}, u32[]{:S(2)}) async-start(bf16[16,32,2048]{2,0,1:T(8,128)(2,1)} %copy.8), calls=%async_computation | async-start | bytes 4194304 | tf_op jit(solution)/shard_map/all_to_all | solution.py:64
where the time goes:
time: 167 us
  blocking collectives  90.6 us (54%)
  starting transfers between devices  28.4 us (17%)
  other arithmetic  23.4 us (14%)
  waiting for transfers between devices  11.2 us (7%)
  local copies, waits for them, and re-layouts  10.5 us (6%)
  matrix products  2.65 us (2%)
    all_gather x1, blocking collectives, local(): lax.all_gather(rotation, 'st', axis=0, tiled=True)  90.6 us
    ppermute x4, waiting for transfers between devices, extended(): lax.ppermute(lax.slice_in_dim(block, block.shape[dim] - width, None, axis...  11.2 us
    all_to_all x1, starting transfers between devices, local(): lax.all_to_all(filtered, 'st', split_axis=1, concat_axis=0, tiled=True)  10.9 us
    sub x2, other arithmetic, chebyshev(): 2.0 * (apply_fn(current) - cheb_shift * current) / cheb_scale - previous  10.8 us
    ppermute x4, starting transfers between devices, extended(): lax.ppermute(lax.slice_in_dim(block, block.shape[dim] - width, None, axis...  9.57 us
    ppermute x4, starting transfers between devices, extended(): lax.ppermute(lax.slice_in_dim(block, 0, width, axis=dim), axis, backward)  7.92 us
    convert_element_type x1, other arithmetic, local(): result.astype(jnp.bfloat16).reshape(states_dev, planes * row_width)  5.77 us
    all_to_all x2, local copies, waits for them, and re-layouts, local(): lax.all_to_all(filtered, 'st', split_axis=1, concat_axis=0, tiled=True)  5.14 us
  transfers between devices with their start and end apart: 9, of which 4 were waited for; matrix products, arithmetic and copies ran while one was open for 1% of the time, Pallas kernels for 0%

commit v1 on v0

--- a/solution.py
+++ b/solution.py
@@ -63,7 +63,9 @@
     filtered = result.astype(jnp.bfloat16).reshape(states_dev, planes * row_width)
     regrouped = lax.all_to_all(filtered, "st", split_axis=1, concat_axis=0, tiled=True)
     product = jnp.dot(
-        lax.all_gather(rotation, "st", axis=0, tiled=True),
+        jnp.concatenate(
+            lax.all_to_all(jnp.stack([rotation] * lax.axis_size("st")), "st", 0, 0), axis=0
+        ),
         regrouped,
         preferred_element_type=jnp.float32,
     )

time: 167 us -> 145 us (0.87)
  blocking collectives: 90.6 us -> 61.1 us
  other arithmetic: 23.4 us -> 33.5 us
  waiting for transfers between devices: 11.2 us -> 8.21 us
    all_gather x1 -> x0, blocking collectives: 90.6 us -> none  [local(): lax.all_gather(rotation, 'st', axis=0, tiled=True)]
    all_to_all x0 -> x1, blocking collectives: none -> 61.1 us  [local(): lax.all_to_all(filtered, 'st', split_axis=1, concat_axis=0, tiled=True)]
    convert_element_type x1, other arithmetic: 5.77 us -> 16 us  [local(): result.astype(jnp.bfloat16).reshape(states_dev, planes * row_width)]
    ppermute x4, waiting for transfers between devices: 11.2 us -> 8.2 us  [extended(): lax.ppermute(lax.slice_in_dim(block, block.shape[dim] - width, None, axis...]
    unnamed x4 -> x8, local copies, waits for them, and re-layouts: 0.01 us -> 1.88 us
  transfers between devices with their start and end apart: 9 -> 9, of which waited for: 4 -> 3; matrix products, arithmetic and copies ran while one was open for 1% -> 15% of each run, Pallas kernels for 0% -> 0%
where the time goes in v1:
time: 145 us; the launch traced here: 144 us
  blocking collectives  61.1 us (42%)
  other arithmetic  33.5 us (23%)
  starting transfers between devices  28.3 us (20%)
  local copies, waits for them, and re-layouts  11.5 us (8%)
  waiting for transfers between devices  8.21 us (6%)
    all_to_all x1, blocking collectives, local(): lax.all_to_all(filtered, 'st', split_axis=1, concat_axis=0, tiled=True)  61.1 us
    convert_element_type x1, other arithmetic, local(): result.astype(jnp.bfloat16).reshape(states_dev, planes * row_width)  16 us
    all_to_all x1, starting transfers between devices, local(): lax.all_to_all(jnp.stack([rotation] * lax.axis_size('st')), 'st', 0, 0)  11.1 us
    sub x2, other arithmetic, chebyshev(): 2.0 * (apply_fn(current) - cheb_shift * current) / cheb_scale - previous  10.8 us
    ppermute x4, starting transfers between devices, extended(): lax.ppermute(lax.slice_in_dim(block, block.shape[dim] - width, None, axis...  9.39 us
    ppermute x4, waiting for transfers between devices, extended(): lax.ppermute(lax.slice_in_dim(block, block.shape[dim] - width, None, axis...  8.2 us
    ppermute x4, starting transfers between devices, extended(): lax.ppermute(lax.slice_in_dim(block, 0, width, axis=dim), axis, backward)  7.91 us
    all_to_all x2, local copies, waits for them, and re-layouts, local(): lax.all_to_all(filtered, 'st', split_axis=1, concat_axis=0, tiled=True)  4.88 us
  transfers between devices with their start and end apart: 9, of which 3 were waited for; matrix products, arithmetic and copies ran while one was open for 15% of the time, Pallas kernels for 0%

profile of v1, /device:TPU:2, one launch (start us, length us, event | category | flops | bytes accessed | tf_op | source)
XLA Modules:
  0.0 144.3 jit_solution(11297244312795342936)
XLA Ops:
  0.0 1.1 fusion.57
  1.2 1.9 %collective-permute-start = (f32[16,1,1024]{2,1,0:T(1,128)S(1)}, f32[16,1,1024]{2,1,0:T(1,128)S(1)}, u32[]{:S(2)}, u32[]{:S(2)}) collective-permute-start(f32[16,1,1024]{2,1,0:T(1,128)S(1)} %get-tuple-element.13), channel_id=1, source_target_pairs={{32,0},{64,32},{96,64},{128,96},{160,128},{192,160},{224,192},{33,... | collective-permute-start | bytes 196616 | tf_op jit(solution)/shard_map/ppermute | solution.py:20
  3.1 2.4 %collective-permute-start.1 = (f32[16,1,1024]{2,1,0:T(1,128)S(1)}, f32[16,1,1024]{2,1,0:T(1,128)S(1)}, u32[]{:S(2)}, u32[]{:S(2)}) collective-permute-start(f32[16,1,1024]{2,1,0:T(1,128)S(1)} %get-tuple-element.14), channel_id=1, source_target_pairs={{0,32},{32,64},{64,96},{96,128},{128,160},{160,192},{192,224},{1,3... | collective-permute-start | bytes 196616 | tf_op jit(solution)/shard_map/ppermute | solution.py:17
  5.5 2.0 %convert_element_type.21 = f32[16,64,1024]{2,1,0:T(8,128)S(1)} convert(bf16[16,64,1024]{2,1,0:T(8,128)(2,1)} %param.3) | non-fusion elementwise | flops 1048576 | bytes 6291456 | tf_op jit(solution)/shard_map/convert_element_type | solution.py:54
  7.6 1.6 %collective-permute-done.1 = f32[16,1,1024]{2,1,0:T(1,128)S(1)} collective-permute-done((f32[16,1,1024]{2,1,0:T(1,128)S(1)}, f32[16,1,1024]{2,1,0:T(1,128)S(1)}, u32[]{:S(2)}, u32[]{:S(2)}) %collective-permute-start.1) | collective-permute-done | bytes 65568 | tf_op jit(solution)/shard_map/ppermute | solution.py:17
  9.3 4.7 %broadcast_multiply_fusion = (f32[16,64,1024]{2,1,0:T(8,128)S(1)}, f32[16,64,1024]{2,1,0:T(8,128)S(1)}) fusion(f32[16,64,1024]{2,1,0:T(8,128)S(1)} %convert_element_type.21, pred[1024]{0:T(1024)(128)(4,1)S(1)} %get-tuple-element.17, pred[1024]{0:T(1024)(128)(4,1)S(1)} %get-tuple-element.18, f32[16,1,1024]{2,1,0:T(1,128)S(1)} %collective-permute-done.1, ...), kind=kLoop, calls=%fused_computation.73 | loop fusion | flops 15728640 | bytes 12978176 | tf_op jit(solution)/shard_map/div | solution.py:45
  14.0 2.2 %collective-permute-start.2 = (f32[16,1,1024]{2,1,0:T(1,128)S(1)}, f32[16,1,1024]{2,1,0:T(1,128)S(1)}, u32[]{:S(2)}, u32[]{:S(2)}) collective-permute-start(f32[16,1,1024]{2,1,0:T(1,128)S(1)} %get-tuple-element.11), channel_id=1, source_target_pairs={{32,0},{64,32},{96,64},{128,96},{160,128},{192,160},{224,192},{33,... | collective-permute-start | bytes 196616 | tf_op jit(solution)/shard_map/ppermute | solution.py:20
  16.2 2.2 %collective-permute-start.3 = (f32[16,1,1024]{2,1,0:T(1,128)S(1)}, f32[16,1,1024]{2,1,0:T(1,128)S(1)}, u32[]{:S(2)}, u32[]{:S(2)}) collective-permute-start(f32[16,1,1024]{2,1,0:T(1,128)S(1)} %get-tuple-element.12), channel_id=1, source_target_pairs={{0,32},{32,64},{64,96},{96,128},{128,160},{160,192},{192,224},{1,3... | collective-permute-start | bytes 196616 | tf_op jit(solution)/shard_map/ppermute | solution.py:17
  18.4 3.4 %collective-permute-done.3 = f32[16,1,1024]{2,1,0:T(1,128)S(1)} collective-permute-done((f32[16,1,1024]{2,1,0:T(1,128)S(1)}, f32[16,1,1024]{2,1,0:T(1,128)S(1)}, u32[]{:S(2)}, u32[]{:S(2)}) %collective-permute-start.3) | collective-permute-done | bytes 65568 | tf_op jit(solution)/shard_map/ppermute | solution.py:17
  21.8 6.1 %fusion.17 = f32[16,64,1024]{2,1,0:T(8,128)S(1)} fusion(f32[16,64,1024]{2,1,0:T(8,128)S(1)} %get-tuple-element.5, f32[16,1,1024]{2,1,0:T(1,128)S(1)} %collective-permute-done.3, f32[16,1,1024]{2,1,0:T(1,128)S(1)} %collective-permute-done.2, f32[16,64,1024]{2,1,0:T(8,128)S(1)} %get-tuple-element.6, f32[64,1024]{1,0:T(8,128)S(1)} %get-tuple-element.15, ...), kind=kLoop, calls=%fused_computation.33 | loop fusion | flops 17825792 | bytes 15075328 | tf_op jit(solution)/shard_map/sub | solution.py:47
  28.0 1.9 %collective-permute-start.4 = (f32[16,1,1024]{2,1,0:T(1,128)S(1)}, f32[16,1,1024]{2,1,0:T(1,128)S(1)}, u32[]{:S(2)}, u32[]{:S(2)}) collective-permute-start(f32[16,1,1024]{2,1,0:T(1,128)S(1)} %get-tuple-element.9), channel_id=1, source_target_pairs={{32,0},{64,32},{96,64},{128,96},{160,128},{192,160},{224,192},{33,... | collective-permute-start | bytes 196616 | tf_op jit(solution)/shard_map/ppermute | solution.py:20
  30.0 2.4 %collective-permute-start.5 = (f32[16,1,1024]{2,1,0:T(1,128)S(1)}, f32[16,1,1024]{2,1,0:T(1,128)S(1)}, u32[]{:S(2)}, u32[]{:S(2)}) collective-permute-start(f32[16,1,1024]{2,1,0:T(1,128)S(1)} %get-tuple-element.10), channel_id=1, source_target_pairs={{0,32},{32,64},{64,96},{96,128},{128,160},{160,192},{192,224},{1,3... | collective-permute-start | bytes 196616 | tf_op jit(solution)/shard_map/ppermute | solution.py:17
  32.4 3.2 %collective-permute-done.5 = f32[16,1,1024]{2,1,0:T(1,128)S(1)} collective-permute-done((f32[16,1,1024]{2,1,0:T(1,128)S(1)}, f32[16,1,1024]{2,1,0:T(1,128)S(1)}, u32[]{:S(2)}, u32[]{:S(2)}) %collective-permute-start.5) | collective-permute-done | bytes 65568 | tf_op jit(solution)/shard_map/ppermute | solution.py:17
  35.6 4.7 %fusion.28 = f32[16,64,1024]{2,1,0:T(8,128)S(1)} fusion(f32[16,64,1024]{2,1,0:T(8,128)S(1)} %fusion.17, f32[16,1,1024]{2,1,0:T(1,128)S(1)} %collective-permute-done.5, f32[16,1,1024]{2,1,0:T(1,128)S(1)} %collective-permute-done.4, f32[16,64,1024]{2,1,0:T(8,128)S(1)} %get-tuple-element.6, f32[64,1024]{1,0:T(8,128)S(1)} %get-tuple-element.16, ...), kind=kLoop, calls=%fused_computation.44 | loop fusion | flops 17825792 | bytes 12978176 | tf_op jit(solution)/shard_map/sub | solution.py:47
  40.4 1.9 %copy-done.1 = f32[16,64,1024]{2,1,0:T(8,128)} copy-done((f32[16,64,1024]{2,1,0:T(8,128)}, f32[16,64,1024]{2,1,0:T(8,128)S(1)}, u32[]{:S(2)}) %copy-start.1) | copy-done | bytes 4194328
  42.3 1.9 %collective-permute-start.6 = (f32[16,1,1024]{2,1,0:T(1,128)S(1)}, f32[16,1,1024]{2,1,0:T(1,128)S(1)}, u32[]{:S(2)}, u32[]{:S(2)}) collective-permute-start(f32[16,1,1024]{2,1,0:T(1,128)S(1)} %get-tuple-element.7), channel_id=1, source_target_pairs={{32,0},{64,32},{96,64},{128,96},{160,128},{192,160},{224,192},{33,... | collective-permute-start | bytes 196616 | tf_op jit(solution)/shard_map/ppermute | solution.py:20
  44.2 2.4 %collective-permute-start.7 = (f32[16,1,1024]{2,1,0:T(1,128)S(1)}, f32[16,1,1024]{2,1,0:T(1,128)S(1)}, u32[]{:S(2)}, u32[]{:S(2)}) collective-permute-start(f32[16,1,1024]{2,1,0:T(1,128)S(1)} %get-tuple-element.8), channel_id=1, source_target_pairs={{0,32},{32,64},{64,96},{96,128},{128,160},{160,192},{192,224},{1,3... | collective-permute-start | bytes 196616 | tf_op jit(solution)/shard_map/ppermute | solution.py:17
  47.5 11.1 %all-to-all-start.1 = ((bf16[32,16,512]{2,1,0:T(8,128)(2,1)}), bf16[32,16,512]{2,1,0:T(8,128)(2,1)S(1)}, u32[]{:S(2)}, u32[]{:S(2)}) async-start(bf16[32,16,512]{2,1,0:T(8,128)(2,1)} %stack.2), calls=%async_computation.1 | async-start | bytes 1048576 | tf_op jit(solution)/shard_map/all_to_all | solution.py:67
  58.6 16.0 %fusion.40 = bf16[16,64,1024]{2,1,0:T(8,128)(2,1)S(1)} fusion(f32[16,64,1024]{2,1,0:T(8,128)} %copy-done, f32[16,64,1024]{2,1,0:T(8,128)} %copy-done.1, f32[16,1,1024]{2,1,0:T(1,128)S(1)} %collective-permute-done.7, f32[16,1,1024]{2,1,0:T(1,128)S(1)} %collective-permute-done.6, f32[64,1024]{1,0:T(8,128)S(1)} %get-tuple-element.16, ...), kind=kLoop, calls=%fused_computation.56 | loop fusion | flops 17825792 | bytes 10881024 | tf_op jit(solution)/shard_map/convert_element_type | solution.py:63
  74.6 2.1 %all_to_all.17 = bf16[16,32,2048]{2,1,0:T(8,128)(2,1)} reshape(bf16[16,64,1024]{2,1,0:T(8,128)(2,1)S(1)} %fusion.40) | data formatting | bytes 4194304 | tf_op jit(solution)/shard_map/all_to_all | solution.py:64
  76.7 2.7 %copy.8 = bf16[16,32,2048]{2,0,1:T(8,128)(2,1)S(1)} copy(bf16[16,32,2048]{2,1,0:T(8,128)(2,1)} %all_to_all.17) | data formatting | bytes 4194304 | tf_op jit(solution)/shard_map/all_to_all | solution.py:64
  79.5 61.1 %all_to_all.24 = bf16[16,32,2048]{2,0,1:T(8,128)(2,1)S(1)} all-to-all(bf16[16,32,2048]{2,0,1:T(8,128)(2,1)S(1)} %copy.8), channel_id=1, replica_groups=mesh['dom'=8,'st'=32] {'st'}, dimensions={1} | all-to-all | bytes 4194304 | tf_op jit(solution)/shard_map/all_to_all | solution.py:64
  140.6 1.3 fusion.47
  141.9 2.4 %copy.9 = bf16[512,2048]{1,0:T(8,128)(2,1)} copy(bf16[512,2048]{0,1:T(8,128)(2,1)S(1)} %fusion.47) | data formatting | bytes 4194304 | tf_op jit(solution)/shard_map/convert_element_type | solution.py:72
  (19 shorter events, 1.3 us)
Async XLA Ops:
  0.0 7.6 %copy-start.2 = (bf16[64,1024]{1,0:T(8,128)(2,1)S(1)}, bf16[64,1024]{1,0:T(8,128)(2,1)}, u32[]{:S(2)}) copy-start(bf16[64,1024]{1,0:T(8,128)(2,1)} %param.4) | copy-start | bytes 393220
  1.2 6.5 %collective-permute-start = (f32[16,1,1024]{2,1,0:T(1,128)S(1)}, f32[16,1,1024]{2,1,0:T(1,128)S(1)}, u32[]{:S(2)}, u32[]{:S(2)}) collective-permute-start(f32[16,1,1024]{2,1,0:T(1,128)S(1)} %get-tuple-element.13), channel_id=1, source_target_pairs={{32,0},{64,32},{96,64},{128,96},{160,128},{192,160},{224,192},{33,... | collective-permute-start | bytes 196616 | tf_op jit(solution)/shard_map/ppermute | solution.py:20
  3.1 6.2 %collective-permute-start.1 = (f32[16,1,1024]{2,1,0:T(1,128)S(1)}, f32[16,1,1024]{2,1,0:T(1,128)S(1)}, u32[]{:S(2)}, u32[]{:S(2)}) collective-permute-start(f32[16,1,1024]{2,1,0:T(1,128)S(1)} %get-tuple-element.14), channel_id=1, source_target_pairs={{0,32},{32,64},{64,96},{96,128},{128,160},{160,192},{192,224},{1,3... | collective-permute-start | bytes 196616 | tf_op jit(solution)/shard_map/ppermute | solution.py:17
  14.0 4.3 %collective-permute-start.2 = (f32[16,1,1024]{2,1,0:T(1,128)S(1)}, f32[16,1,1024]{2,1,0:T(1,128)S(1)}, u32[]{:S(2)}, u32[]{:S(2)}) collective-permute-start(f32[16,1,1024]{2,1,0:T(1,128)S(1)} %get-tuple-element.11), channel_id=1, source_target_pairs={{32,0},{64,32},{96,64},{128,96},{160,128},{192,160},{224,192},{33,... | collective-permute-start | bytes 196616 | tf_op jit(solution)/shard_map/ppermute | solution.py:20
  16.2 5.6 %collective-permute-start.3 = (f32[16,1,1024]{2,1,0:T(1,128)S(1)}, f32[16,1,1024]{2,1,0:T(1,128)S(1)}, u32[]{:S(2)}, u32[]{:S(2)}) collective-permute-start(f32[16,1,1024]{2,1,0:T(1,128)S(1)} %get-tuple-element.12), channel_id=1, source_target_pairs={{0,32},{32,64},{64,96},{96,128},{128,160},{160,192},{192,224},{1,3... | collective-permute-start | bytes 196616 | tf_op jit(solution)/shard_map/ppermute | solution.py:17
  27.9 12.4 %copy-start = (f32[16,64,1024]{2,1,0:T(8,128)}, f32[16,64,1024]{2,1,0:T(8,128)S(1)}, u32[]{:S(2)}) copy-start(f32[16,64,1024]{2,1,0:T(8,128)S(1)} %fusion.17) | copy-start | bytes 12582916
  28.0 4.4 %collective-permute-start.4 = (f32[16,1,1024]{2,1,0:T(1,128)S(1)}, f32[16,1,1024]{2,1,0:T(1,128)S(1)}, u32[]{:S(2)}, u32[]{:S(2)}) collective-permute-start(f32[16,1,1024]{2,1,0:T(1,128)S(1)} %get-tuple-element.9), channel_id=1, source_target_pairs={{32,0},{64,32},{96,64},{128,96},{160,128},{192,160},{224,192},{33,... | collective-permute-start | bytes 196616 | tf_op jit(solution)/shard_map/ppermute | solution.py:20
  30.0 16.6 %copy-start.3 = (bf16[16,512]{1,0:T(8,128)(2,1)S(1)}, bf16[16,512]{1,0:T(8,128)(2,1)}, u32[]{:S(2)}) copy-start(bf16[16,512]{1,0:T(8,128)(2,1)} %param.5) | copy-start | bytes 49156
  30.0 5.6 %collective-permute-start.5 = (f32[16,1,1024]{2,1,0:T(1,128)S(1)}, f32[16,1,1024]{2,1,0:T(1,128)S(1)}, u32[]{:S(2)}, u32[]{:S(2)}) collective-permute-start(f32[16,1,1024]{2,1,0:T(1,128)S(1)} %get-tuple-element.10), channel_id=1, source_target_pairs={{0,32},{32,64},{64,96},{96,128},{128,160},{160,192},{192,224},{1,3... | collective-permute-start | bytes 196616 | tf_op jit(solution)/shard_map/ppermute | solution.py:17
  40.3 2.0 %copy-start.1 = (f32[16,64,1024]{2,1,0:T(8,128)}, f32[16,64,1024]{2,1,0:T(8,128)S(1)}, u32[]{:S(2)}) copy-start(f32[16,64,1024]{2,1,0:T(8,128)S(1)} %fusion.28) | copy-start | bytes 12582916
  42.3 16.3 %collective-permute-start.6 = (f32[16,1,1024]{2,1,0:T(1,128)S(1)}, f32[16,1,1024]{2,1,0:T(1,128)S(1)}, u32[]{:S(2)}, u32[]{:S(2)}) collective-permute-start(f32[16,1,1024]{2,1,0:T(1,128)S(1)} %get-tuple-element.7), channel_id=1, source_target_pairs={{32,0},{64,32},{96,64},{128,96},{160,128},{192,160},{224,192},{33,... | collective-permute-start | bytes 196616 | tf_op jit(solution)/shard_map/ppermute | solution.py:20
  44.2 14.4 %collective-permute-start.7 = (f32[16,1,1024]{2,1,0:T(1,128)S(1)}, f32[16,1,1024]{2,1,0:T(1,128)S(1)}, u32[]{:S(2)}, u32[]{:S(2)}) collective-permute-start(f32[16,1,1024]{2,1,0:T(1,128)S(1)} %get-tuple-element.8), channel_id=1, source_target_pairs={{0,32},{32,64},{64,96},{96,128},{128,160},{160,192},{192,224},{1,3... | collective-permute-start | bytes 196616 | tf_op jit(solution)/shard_map/ppermute | solution.py:17
  47.5 32.0 %all-to-all-start.1 = ((bf16[32,16,512]{2,1,0:T(8,128)(2,1)}), bf16[32,16,512]{2,1,0:T(8,128)(2,1)S(1)}, u32[]{:S(2)}, u32[]{:S(2)}) async-start(bf16[32,16,512]{2,1,0:T(8,128)(2,1)} %stack.2), calls=%async_computation.1 | async-start | bytes 1048576 | tf_op jit(solution)/shard_map/all_to_all | solution.py:67
